TPU v7x, 32 devices: a whole 2x2x4 slice. The times are simulated.
32 devices in a mesh: fsdp: 8 (over z, x), seq: 4 (over y, core).
Axes of the slice: x: 2, y: 2, z: 4, core: 2. Of those that a mesh axis runs over, the one named last changes fastest.
Arguments:
- context: bfloat16 [16, 512, 2560], P('fsdp', 'seq'), may hold values from -6 to 6
- residual: bfloat16 [16, 512, 2560], P('fsdp', 'seq'), may hold values from -6 to 6
- target_rows: bfloat16 [16, 512, 2560], P('fsdp', 'seq'), may hold values from -0.00390625 to 0.00390625
- log_norm: float32 [16, 512], P('fsdp', 'seq'), may hold values from -0.15 to 0.15
- norm_gain: float32 [2560], replicated, may hold values from 0.1 to 1.9
- out_proj: bfloat16 [2560, 2560], P('fsdp'), may hold values from -0.125 to 0.125
- old_logprob: float32 [16, 512], P('fsdp', 'seq'), may hold values from -0.15 to 0.15
- lengths: int32 [16, 4], P('fsdp', 'seq'), may hold values from 112 to 128
- rewards: float32 [16, 4], P('fsdp', 'seq'), may hold values from -5 to 5
- prompt_ids: int32 [16, 4], P('fsdp', 'seq'), may hold values from 0 to 3, as said below
- placement: int32 [16, 4], P('fsdp', 'seq'), may hold values from 0 to 15, as said below
Outputs:
- grad_context: bfloat16 [16, 512, 2560], P('fsdp', 'seq')
- grad_weight: float32 [2560, 2560], P('fsdp')
- loss: float32 [], replicated
Inputs may be any that keep to these rules, and one draw needn't show every extreme that they name: `prompt_ids`: every prompt id names exactly 16 rows. Sampler row (a, s) goes to learner row (placement[a, s], s) and keeps a mod 2; the 2 rows of one device go to 2 different fsdp indices; every learner row receives exactly one row; in every column one of the 2 rows of each device goes 8 / 2 fsdp indices onward and another goes 1 index onward, counted round.
All inputs are finite; a program needn't handle non-finite values.
Results may differ from a plain program's by a relative error of at most 0.014.
Values may be sent and summed in bfloat16 or wider, within the bound.
A program may use at most 128 MiB of HBM per device.

v0:
```python
import math
import jax
import jax.numpy as jnp
from jax import lax
from jax.sharding import PartitionSpec as P

DW = 2560
AW = 2560
GS = 16


def body(
    context,
    residual,
    target_rows,
    log_norm,
    norm_gain,
    out_proj,
    old_logprob,
    lengths,
    rewards,
    prompt_ids,
    placement,
):
    nrows = context.shape[0]
    lmax = context.shape[1]
    fsdp_ways = lax.axis_size("fsdp")
    seq_ways = lax.axis_size("seq")
    prompts = nrows * fsdp_ways * seq_ways // GS
    all_tokens = nrows * lmax * fsdp_ways * seq_ways
    reward_flat = rewards.reshape(-1)
    prompt_flat = prompt_ids.reshape(-1)
    length_flat = lengths.reshape(-1)
    dest_flat = placement.reshape(-1)
    prompt_range = jnp.arange(prompts, dtype=jnp.int32)
    local_hot = (prompt_flat[:, None] == prompt_range[None, :]).astype(jnp.float32)
    group_sum, group_sq, count = lax.psum(
        (
            jnp.sum(local_hot * reward_flat[:, None], axis=0),
            jnp.sum(local_hot * (reward_flat * reward_flat)[:, None], axis=0),
            jnp.sum(length_flat.astype(jnp.float32)),
        ),
        ("fsdp", "seq"),
    )
    group_mean = group_sum / GS
    group_var = group_sq / GS - group_mean * group_mean
    row_mean = jnp.sum(local_hot * group_mean[None, :], axis=1)
    row_var = jnp.sum(local_hot * group_var[None, :], axis=1)
    advantage = (reward_flat - row_mean) / jnp.sqrt(row_var + 0.25)
    slots = jnp.arange(nrows, dtype=jnp.int32)
    every_old, every_adv, every_len, every_dest = (
        lax.all_gather(old_logprob, "fsdp", axis=0, tiled=True),
        lax.all_gather(advantage, "fsdp", axis=0, tiled=True),
        lax.all_gather(length_flat, "fsdp", axis=0, tiled=True),
        lax.all_gather(dest_flat, "fsdp", axis=0, tiled=True),
    )
    wanted = lax.axis_index("fsdp") * nrows + slots
    chosen = every_dest[None, :] == wanted[:, None]
    learn_old = jnp.sum(jnp.where(chosen[:, :, None], every_old[None, :, :], 0.0), axis=1)
    learn_adv = jnp.sum(jnp.where(chosen, every_adv[None, :], 0.0), axis=1)
    learn_len = jnp.sum(jnp.where(chosen, every_len[None, :], 0), axis=1)
    offsets = jnp.arange(lmax, dtype=jnp.int32)
    valid = (offsets[None, :] < learn_len[:, None]).astype(jnp.float32).reshape(-1)
    token_adv = jnp.broadcast_to(learn_adv[:, None], (nrows, lmax)).reshape(-1)
    tokens = nrows * lmax
    context_flat = context.reshape(tokens, AW)
    whole = lax.all_gather(out_proj, "fsdp", axis=0, tiled=True)
    hidden = residual.reshape(tokens, DW).astype(jnp.float32) + jnp.dot(
        context_flat, whole, preferred_element_type=jnp.float32
    )
    rinv = lax.rsqrt(jnp.mean(hidden * hidden, axis=1) + 1e-06)
    vecs = norm_gain[None, :] * target_rows.reshape(tokens, DW).astype(jnp.float32)
    hv_sum = jnp.sum(hidden * vecs, axis=1)
    score = hv_sum * rinv
    ratio = jnp.exp(score - log_norm.reshape(-1) - learn_old.reshape(-1))
    plain = ratio * token_adv
    clipped = jnp.clip(ratio, 0.8, 1.2) * token_adv
    objective = jnp.minimum(plain, clipped)
    loss_local = jnp.sum(valid * -objective)
    dscore = -valid * jnp.where(plain <= clipped, plain, 0.0) / count
    dhid = (dscore * rinv)[:, None] * (vecs - hidden * (rinv * rinv * hv_sum / DW)[:, None])
    grad_hidden = (dhid * (32.0 * all_tokens * math.sqrt(DW))).astype(jnp.bfloat16)
    grad_context = lax.dot_general(
        grad_hidden, whole, (((1,), (1,)), ((), ())), preferred_element_type=jnp.float32
    ).astype(jnp.bfloat16)
    piece = lax.psum_scatter(
        lax.dot_general(
            context_flat, grad_hidden, (((0,), (0,)), ((), ())), preferred_element_type=jnp.float32
        ).astype(jnp.bfloat16),
        "fsdp",
        scatter_dimension=0,
        tiled=True,
    )
    grad_weight = lax.psum(piece, "seq").astype(jnp.float32) * (1.0 / math.sqrt(all_tokens))
    loss = lax.psum(loss_local, ("fsdp", "seq")) / count
    return (grad_context.reshape(nrows, lmax, AW), grad_weight, loss)


def solution(mesh):
    return jax.shard_map(
        body,
        mesh=mesh,
        in_specs=(
            P("fsdp", "seq", None),
            P("fsdp", "seq", None),
            P("fsdp", "seq", None),
            P("fsdp", "seq"),
            P(),
            P("fsdp", None),
            P("fsdp", "seq"),
            P("fsdp", "seq"),
            P("fsdp", "seq"),
            P("fsdp", "seq"),
            P("fsdp", "seq"),
        ),
        out_specs=(P("fsdp", "seq", None), P("fsdp", None), P()),
        check_vma=False,
    )
```

profile of v0, /device:TPU:0, one launch (start us, length us, event | category | flops | bytes accessed | tf_op | source)
XLA Modules:
  0.0 559.2 jit_solution(6872598172934750625)
XLA Ops:
  7.2 0.0 copy-start
  7.2 0.0 all-gather.5.cloned.1.call-start
  7.2 0.7 all-gather.5.cloned.1.call-update
  7.9 0.0 reduce-scatter.4.cloned.1.call-start
  8.0 0.7 multiply_bitcast_fusion
  8.6 0.8 select_reduce_fusion.6
  9.4 46.3 %all-reduce.5 = (f32[4]{0:T(128)S(1)}, f32[4]{0:T(128)S(1)}) all-reduce(f32[4]{0:T(128)S(1)} %get-tuple-element.16, f32[4]{0:T(128)S(1)} %get-tuple-element.17), channel_id=1, replica_groups=mesh['fsdp'=8,'seq'=4] {'fsdp','seq'}, use_global_device_ids=true, to_apply=%region_5.0 | all-reduce | flops 8 | bytes 64 | tf_op jit(solution)/shard_map/psum | solution.py:37
  55.7 1.2 dynamic-slice
  57.6 0.9 select_reduce_fusion.5
  58.5 0.8 bitcast_dynamic-update-slice_fusion.1
  59.2 0.7 multiply_dynamic-update-slice_fusion
  60.0 0.7 bitcast_dynamic-update-slice_fusion
  60.7 20.1 %all-reduce.2 = f32[16]{0:T(128)S(1)} all-reduce(f32[16]{0:T(128)S(1)} %multiply_dynamic-update-slice_fusion), channel_id=1, replica_groups=mesh['fsdp'=8,'seq'=4] {'fsdp'}, use_global_device_ids=true, to_apply=%add.2 | all-reduce | flops 16 | bytes 128
  80.9 12.8 %all-reduce.3 = (s32[16]{0:T(128)S(1)}, s32[16]{0:T(128)S(1)}) all-reduce(s32[16]{0:T(128)S(1)} %bitcast_dynamic-update-slice_fusion.1, s32[16]{0:T(128)S(1)} %bitcast_dynamic-update-slice_fusion), channel_id=2, replica_groups=mesh['fsdp'=8,'seq'=4] {'fsdp'}, use_global_device_ids=true, to_apply=%add | all-reduce | flops 32 | bytes 256
  93.7 18.2 %all-gather.2 = f32[8,2,128]{2,1,0:T(2,128)S(1)} all-gather(f32[1,2,128]{2,1,0:T(2,128)} %bitcast.68), channel_id=1, replica_groups=mesh['fsdp'=8,'seq'=4] {'fsdp'}, dimensions={0}, use_global_device_ids=true | all-gather | bytes 9216 | tf_op jit(solution)/shard_map/all_gather | solution.py:52
  111.9 1.3 convert_reduce_fusion
  113.1 0.2 select_reduce_fusion.2
  113.3 0.1 select_reduce_fusion.7
  113.4 0.1 select_reduce_fusion
  113.5 83.5 %all-gather.5.cloned.1.call-done = bf16[2560,2560]{1,0:T(8,128)(2,1)} async-done(((bf16[320,2560]{1,0:T(8,128)(2,1)}), bf16[2560,2560]{1,0:T(8,128)(2,1)}) %all-gather.5.cloned.1.call-update) | async-done | bytes 13107216 | tf_op jit(solution)/shard_map/all_gather | solution.py:67
  197.0 0.0 copy-done
  197.0 0.0 copy-start.2
  197.0 0.0 copy-start.1
  197.0 10.4 %multiply_reduce_fusion = (f32[256]{0:T(256)S(1)}, f32[256]{0:T(256)S(1)}, f32[256,2560]{1,0:T(8,128)}) fusion(bf16[2,128,2560]{2,1,0:T(8,128)(2,1)} %param.13, f32[2560]{0:T(1024)} %param.15, bf16[256,2560]{1,0:T(8,128)(2,1)S(1)} %bitcast.62, bf16[2560,2560]{1,0:T(8,128)(2,1)} %all-gather.5.cloned.1.call-done, bf16[256,2560]{1,0:T(8,128)(2,1)} %bitcast.69), kind=kOutput, calls=%fused_computation.12 | convolution fusion | flops 3360685568 | bytes 19673088 | tf_op jit(solution)/shard_map/dot_general | solution.py:68
  207.4 0.0 copy-done.2
  207.4 0.7 select_reduce_fusion.1
  208.1 38.7 %all-reduce.4 = (f32[]{:T(128)}, f32[]{:T(128)}) all-reduce(f32[]{:T(128)} %convert_reduce_fusion, f32[]{:T(128)} %select_reduce_fusion.1), channel_id=1, replica_groups=mesh['fsdp'=8,'seq'=4] {'fsdp','seq'}, use_global_device_ids=true, to_apply=%region_12.13 | all-reduce | flops 2 | bytes 16 | tf_op jit(solution)/shard_map/psum | solution.py:37
  246.7 0.7 divide_multiply_fusion
  247.5 0.0 copy-done.1
  247.5 2.7 fusion.6
  250.2 6.8 %fusion = bf16[2560,2560]{0,1:T(8,128)(2,1)} fusion(bf16[256,2560]{1,0:T(8,128)(2,1)S(1)} %fusion.6, bf16[256,2560]{1,0:T(8,128)(2,1)S(1)} %bitcast.63), kind=kOutput, calls=%fused_computation.1 | convolution fusion | flops 3361996800 | bytes 15728640 | tf_op jit(solution)/shard_map/dot_general | solution.py:87
  257.0 17.6 %copy.17 = bf16[2560,2560]{1,0:T(8,128)(2,1)} copy(bf16[2560,2560]{0,1:T(8,128)(2,1)} %fusion) | data formatting | bytes 26214400
  274.6 0.0 reduce-scatter.4.cloned.1.call-update
  274.6 0.0 all-reduce.8.cloned.1.call-start
  276.0 214.2 %reduce-scatter.4.cloned.1.call-done = bf16[320,2560]{1,0:T(8,128)(2,1)} async-done(((bf16[2560,2560]{1,0:T(8,128)(2,1)}), bf16[320,2560]{1,0:T(8,128)(2,1)}) %reduce-scatter.4.cloned.1.call-update) | async-done | bytes 1638416
  490.2 3.8 copy.18
  494.0 0.0 all-reduce.8.cloned.1.call-update
  494.0 9.4 %convolution_convert_fusion.1 = bf16[256,2560]{1,0:T(8,128)(2,1)} fusion(bf16[256,2560]{1,0:T(8,128)(2,1)S(1)} %fusion.6, bf16[2560,2560]{1,0:T(8,128)(2,1)} %all-gather.5.cloned.1.call-done), kind=kOutput, calls=%fused_computation.4 | convolution fusion | flops 3356098560 | bytes 15728640 | tf_op jit(solution)/shard_map/dot_general | solution.py:83
  503.4 39.1 %all-reduce.8.cloned.1.call-done = bf16[320,2560]{0,1:T(8,128)(2,1)} async-done(((bf16[320,2560]{0,1:T(8,128)(2,1)}), bf16[320,2560]{0,1:T(8,128)(2,1)}) %all-reduce.8.cloned.1.call-update) | async-done | bytes 1638416 | tf_op jit(solution)/shard_map/psum | solution.py:94
  542.6 3.8 convert_multiply_fusion
  546.3 5.2 copy.16
  (5 shorter events, 0.0 us)
Async XLA Ops:
  7.2 189.9 %copy-start = (bf16[2,128,2560]{2,1,0:T(8,128)(2,1)S(1)}, bf16[2,128,2560]{2,1,0:T(8,128)(2,1)}, u32[]{:S(2)}) copy-start(bf16[2,128,2560]{2,1,0:T(8,128)(2,1)} %param.11) | copy-start | bytes 3932164
  7.2 189.9 %all-gather.5.cloned.1.call-start = ((), (), s32[]{:S(2)}) async-start(), calls=%async_computation.1 | async-start | bytes 14745600 | tf_op jit(solution)/shard_map/all_gather | solution.py:67
  7.9 482.3 %reduce-scatter.4.cloned.1.call-start = ((), (), s32[]{:S(2)}) async-start(), calls=%async_computation.3 | async-start | bytes 14745600
  197.0 10.4 %copy-start.2 = (f32[2,128]{1,0:T(2,128)S(1)}, f32[2,128]{1,0:T(2,128)}, u32[]{:S(2)}) copy-start(f32[2,128]{1,0:T(2,128)} %param.14) | copy-start | bytes 3076
  197.0 50.4 %copy-start.1 = (f32[2560]{0:T(1024)S(1)}, f32[2560]{0:T(1024)}, u32[]{:S(2)}) copy-start(f32[2560]{0:T(1024)} %param.15) | copy-start | bytes 30724
  274.6 267.9 %all-reduce.8.cloned.1.call-start = ((), (), s32[]{:S(2)}) async-start(), calls=%async_computation.2 | async-start | bytes 3932160 | tf_op jit(solution)/shard_map/psum | solution.py:94
Sparse Core Ops, SparseCore 0:
  10.2 186.7 all-gather.4
  274.7 215.4 reduce-scatter.3
  494.2 48.3 all-reduce.7
where the time goes:
time: 560 us; the launch traced here: 559 us
  waiting for transfers between devices  338 us (60%)
  blocking collectives  136 us (24%)
  local copies, waits for them, and re-layouts  29.4 us (5%)
  matrix products  26.5 us (5%)
  between operations  16.9 us (3%)
  other arithmetic  12.6 us (2%)
    unnamed x4, waiting for transfers between devices  215 us
    psum x2, blocking collectives, body(): lax.psum((jnp.sum(local_hot * reward_flat[:, None], axis=0), jnp.sum(loca...  85 us
    all_gather x1, waiting for transfers between devices, body(): whole = lax.all_gather(out_proj, 'fsdp', axis=0, tiled=True)  83.5 us
    psum x1, waiting for transfers between devices, body(): lax.psum(piece, 'seq').astype(jnp.float32) * (1.0 / math.sqrt(all_tokens))  39.1 us
    unnamed x2, blocking collectives  33 us
    unnamed x15, local copies, waits for them, and re-layouts  29.4 us
    all_gather x1, blocking collectives, body(): lax.all_gather(old_logprob, 'fsdp', axis=0, tiled=True)  18.2 us
  transfers between devices with their start and end apart: 3, of which 3 were waited for; matrix products, arithmetic and copies ran while one was open for 3% of the time, Pallas kernels for 0%

commit v1 on v0

--- a/solution.py
+++ b/solution.py
@@ -49,7 +49,9 @@
     advantage = (reward_flat - row_mean) / jnp.sqrt(row_var + 0.25)
     slots = jnp.arange(nrows, dtype=jnp.int32)
     every_old, every_adv, every_len, every_dest = (
-        lax.all_gather(old_logprob, "fsdp", axis=0, tiled=True),
+        jnp.concatenate(
+            lax.all_to_all(jnp.stack([old_logprob] * lax.axis_size("fsdp")), "fsdp", 0, 0), axis=0
+        ),
         lax.all_gather(advantage, "fsdp", axis=0, tiled=True),
         lax.all_gather(length_flat, "fsdp", axis=0, tiled=True),
         lax.all_gather(dest_flat, "fsdp", axis=0, tiled=True),

time: 560 us -> 560 us (level)
  blocking collectives: 136 us -> 111 us
  waiting for transfers between devices: 338 us -> 354 us
  starting transfers between devices: 0.12 us -> 7.37 us
    all_gather x1 -> x0, blocking collectives: 18.2 us -> none  [body(): lax.all_gather(old_logprob, 'fsdp', axis=0, tiled=True)]
    all_gather x1, waiting for transfers between devices: 83.5 us -> 100 us  [body(): whole = lax.all_gather(out_proj, 'fsdp', axis=0, tiled=True)]
    all_to_all x0 -> x1, starting transfers between devices: none -> 7.25 us  [body(): lax.all_to_all(jnp.stack([old_logprob] * lax.axis_size('fsdp')), 'fsdp',...]
    unnamed x2, blocking collectives: 33 us -> 26.7 us
  transfers between devices with their start and end apart: 3 -> 4, of which waited for: 3 -> 3; matrix products, arithmetic and copies ran while one was open for 3% -> 3% of each run, Pallas kernels for 0% -> 0%
where the time goes in v1:
time: 560 us; the launch traced here: 559 us
  waiting for transfers between devices  354 us (63%)
  blocking collectives  111 us (20%)
  local copies, waits for them, and re-layouts  30.7 us (5%)
  matrix products  26.6 us (5%)
  between operations  16.9 us (3%)
  other arithmetic  12.6 us (2%)
  starting transfers between devices  7.37 us (1%)
    unnamed x4, waiting for transfers between devices  215 us
    all_gather x1, waiting for transfers between devices, body(): whole = lax.all_gather(out_proj, 'fsdp', axis=0, tiled=True)  100 us
    psum x2, blocking collectives, body(): lax.psum((jnp.sum(local_hot * reward_flat[:, None], axis=0), jnp.sum(loca...  84.2 us
    psum x1, waiting for transfers between devices, body(): lax.psum(piece, 'seq').astype(jnp.float32) * (1.0 / math.sqrt(all_tokens))  39.1 us
    unnamed x15, local copies, waits for them, and re-layouts  29.4 us
    unnamed x2, blocking collectives  26.7 us
  transfers between devices with their start and end apart: 4, of which 3 were waited for; matrix products, arithmetic and copies ran while one was open for 3% of the time, Pallas kernels for 0%

profile of v1, /device:TPU:0, one launch (start us, length us, event | category | flops | bytes accessed | tf_op | source)
XLA Modules:
  0.0 559.1 jit_solution(15463113069425308905)
XLA Ops:
  7.2 0.0 copy-start
  7.2 0.0 all-gather.4.cloned.1.call-start
  7.2 0.7 all-gather.4.cloned.1.call-update
  7.9 1.3 stack.2
  9.2 7.3 %all-to-all-start = ((f32[8,2,128]{2,1,0:T(2,128)}), f32[8,2,128]{2,1,0:T(2,128)S(1)}, u32[]{:S(2)}, u32[]{:S(2)}) async-start(f32[8,2,128]{2,1,0:T(2,128)} %stack.2), calls=%async_computation | async-start | bytes 16384 | tf_op jit(solution)/shard_map/all_to_all | solution.py:53
  16.4 0.0 reduce-scatter.4.cloned.1.call-start
  16.5 0.7 multiply_bitcast_fusion
  17.2 0.8 select_reduce_fusion.6
  17.9 45.5 %all-reduce.5 = (f32[4]{0:T(128)S(1)}, f32[4]{0:T(128)S(1)}) all-reduce(f32[4]{0:T(128)S(1)} %get-tuple-element.16, f32[4]{0:T(128)S(1)} %get-tuple-element.17), channel_id=1, replica_groups=mesh['fsdp'=8,'seq'=4] {'fsdp','seq'}, use_global_device_ids=true, to_apply=%region_5.0 | all-reduce | flops 8 | bytes 64 | tf_op jit(solution)/shard_map/psum | solution.py:37
  63.4 1.2 dynamic-slice
  65.3 0.9 select_reduce_fusion.5
  66.2 0.8 bitcast_dynamic-update-slice_fusion.1
  66.9 0.7 multiply_dynamic-update-slice_fusion
  67.7 0.7 bitcast_dynamic-update-slice_fusion
  68.4 19.9 %all-reduce.2 = f32[16]{0:T(128)S(1)} all-reduce(f32[16]{0:T(128)S(1)} %multiply_dynamic-update-slice_fusion), channel_id=1, replica_groups=mesh['fsdp'=8,'seq'=4] {'fsdp'}, use_global_device_ids=true, to_apply=%add.2 | all-reduce | flops 16 | bytes 128
  88.4 6.8 %all-reduce.3 = (s32[16]{0:T(128)S(1)}, s32[16]{0:T(128)S(1)}) all-reduce(s32[16]{0:T(128)S(1)} %bitcast_dynamic-update-slice_fusion.1, s32[16]{0:T(128)S(1)} %bitcast_dynamic-update-slice_fusion), channel_id=2, replica_groups=mesh['fsdp'=8,'seq'=4] {'fsdp'}, use_global_device_ids=true, to_apply=%add | all-reduce | flops 32 | bytes 256
  95.2 0.2 select_reduce_fusion.2
  95.3 0.1 select_reduce_fusion.7
  95.5 1.3 convert_reduce_fusion
  96.7 0.0 all-to-all-done
  96.7 0.1 select_reduce_fusion
  96.8 100.1 %all-gather.4.cloned.1.call-done = bf16[2560,2560]{1,0:T(8,128)(2,1)} async-done(((bf16[320,2560]{1,0:T(8,128)(2,1)}), bf16[2560,2560]{1,0:T(8,128)(2,1)}) %all-gather.4.cloned.1.call-update) | async-done | bytes 13107216 | tf_op jit(solution)/shard_map/all_gather | solution.py:69
  196.9 0.0 copy-done
  196.9 0.0 copy-start.2
  196.9 0.0 copy-start.1
  196.9 10.4 %multiply_reduce_fusion = (f32[256]{0:T(256)S(1)}, f32[256]{0:T(256)S(1)}, f32[256,2560]{1,0:T(8,128)}) fusion(bf16[2,128,2560]{2,1,0:T(8,128)(2,1)} %param.13, f32[2560]{0:T(1024)} %param.15, bf16[256,2560]{1,0:T(8,128)(2,1)S(1)} %bitcast.61, bf16[2560,2560]{1,0:T(8,128)(2,1)} %all-gather.4.cloned.1.call-done, bf16[256,2560]{1,0:T(8,128)(2,1)} %bitcast.67), kind=kOutput, calls=%fused_computation.12 | convolution fusion | flops 3360685568 | bytes 19673088 | tf_op jit(solution)/shard_map/dot_general | solution.py:70
  207.3 0.0 copy-done.2
  207.3 0.7 select_reduce_fusion.1
  207.9 38.7 %all-reduce.4 = (f32[]{:T(128)}, f32[]{:T(128)}) all-reduce(f32[]{:T(128)} %convert_reduce_fusion, f32[]{:T(128)} %select_reduce_fusion.1), channel_id=1, replica_groups=mesh['fsdp'=8,'seq'=4] {'fsdp','seq'}, use_global_device_ids=true, to_apply=%region_12.13 | all-reduce | flops 2 | bytes 16 | tf_op jit(solution)/shard_map/psum | solution.py:37
  246.6 0.7 divide_multiply_fusion
  247.3 0.0 copy-done.1
  247.3 2.7 fusion.6
  250.1 6.8 %fusion = bf16[2560,2560]{0,1:T(8,128)(2,1)} fusion(bf16[256,2560]{1,0:T(8,128)(2,1)S(1)} %fusion.6, bf16[256,2560]{1,0:T(8,128)(2,1)S(1)} %bitcast.62), kind=kOutput, calls=%fused_computation.1 | convolution fusion | flops 3361996800 | bytes 15728640 | tf_op jit(solution)/shard_map/dot_general | solution.py:89
  256.8 17.6 %copy.17 = bf16[2560,2560]{1,0:T(8,128)(2,1)} copy(bf16[2560,2560]{0,1:T(8,128)(2,1)} %fusion) | data formatting | bytes 26214400
  274.5 0.0 reduce-scatter.4.cloned.1.call-update
  274.5 0.0 all-reduce.8.cloned.1.call-start
  275.9 214.3 %reduce-scatter.4.cloned.1.call-done = bf16[320,2560]{1,0:T(8,128)(2,1)} async-done(((bf16[2560,2560]{1,0:T(8,128)(2,1)}), bf16[320,2560]{1,0:T(8,128)(2,1)}) %reduce-scatter.4.cloned.1.call-update) | async-done | bytes 1638416
  490.1 3.8 copy.18
  494.0 0.0 all-reduce.8.cloned.1.call-update
  494.0 9.4 %convolution_convert_fusion.1 = bf16[256,2560]{1,0:T(8,128)(2,1)} fusion(bf16[256,2560]{1,0:T(8,128)(2,1)S(1)} %fusion.6, bf16[2560,2560]{1,0:T(8,128)(2,1)} %all-gather.4.cloned.1.call-done), kind=kOutput, calls=%fused_computation.4 | convolution fusion | flops 3356098560 | bytes 15728640 | tf_op jit(solution)/shard_map/dot_general | solution.py:85
  503.4 39.1 %all-reduce.8.cloned.1.call-done = bf16[320,2560]{0,1:T(8,128)(2,1)} async-done(((bf16[320,2560]{0,1:T(8,128)(2,1)}), bf16[320,2560]{0,1:T(8,128)(2,1)}) %all-reduce.8.cloned.1.call-update) | async-done | bytes 1638416 | tf_op jit(solution)/shard_map/psum | solution.py:96
  542.5 3.8 convert_multiply_fusion
  546.2 5.2 copy.16
  (5 shorter events, 0.0 us)
Async XLA Ops:
  7.2 189.7 %copy-start = (bf16[2,128,2560]{2,1,0:T(8,128)(2,1)S(1)}, bf16[2,128,2560]{2,1,0:T(8,128)(2,1)}, u32[]{:S(2)}) copy-start(bf16[2,128,2560]{2,1,0:T(8,128)(2,1)} %param.11) | copy-start | bytes 3932164
  7.2 189.7 %all-gather.4.cloned.1.call-start = ((), (), s32[]{:S(2)}) async-start(), calls=%async_computation.2 | async-start | bytes 14745600 | tf_op jit(solution)/shard_map/all_gather | solution.py:69
  9.2 87.5 %all-to-all-start = ((f32[8,2,128]{2,1,0:T(2,128)}), f32[8,2,128]{2,1,0:T(2,128)S(1)}, u32[]{:S(2)}, u32[]{:S(2)}) async-start(f32[8,2,128]{2,1,0:T(2,128)} %stack.2), calls=%async_computation | async-start | bytes 16384 | tf_op jit(solution)/shard_map/all_to_all | solution.py:53
  16.4 473.7 %reduce-scatter.4.cloned.1.call-start = ((), (), s32[]{:S(2)}) async-start(), calls=%async_computation.4 | async-start | bytes 14745600
  196.9 10.4 %copy-start.2 = (f32[2,128]{1,0:T(2,128)S(1)}, f32[2,128]{1,0:T(2,128)}, u32[]{:S(2)}) copy-start(f32[2,128]{1,0:T(2,128)} %param.14) | copy-start | bytes 3076
  196.9 50.4 %copy-start.1 = (f32[2560]{0:T(1024)S(1)}, f32[2560]{0:T(1024)}, u32[]{:S(2)}) copy-start(f32[2560]{0:T(1024)} %param.15) | copy-start | bytes 30724
  274.5 268.0 %all-reduce.8.cloned.1.call-start = ((), (), s32[]{:S(2)}) async-start(), calls=%async_computation.3 | async-start | bytes 3932160 | tf_op jit(solution)/shard_map/psum | solution.py:96
Sparse Core Ops, SparseCore 0:
  10.2 186.6 all-gather.3
  274.6 215.4 reduce-scatter.3
  494.1 48.3 all-reduce.7
